TPU v7x, 512 devices: a whole 4x8x8 slice. The times are simulated.
512 devices in a mesh: row: 32 (over y_hi, x, core), col: 16 (over z, y_lo).
Axes of the slice: x: 4, y: 8 (y_hi: 4, y_lo: 2; y = y_hi * 2 + y_lo), z: 8, core: 2. Of those that a mesh axis runs over, the one named last changes fastest.
Arguments:
- density: float32 [4096, 4096], P('row', 'col'), may hold values from -1 to 1, as said below
- pattern: int32 [32, 32], P('row', 'col'), may hold values from 0 to 1, as said below
- step_choices: int32 [2], replicated, may hold values from 0 to 1, as said below
Outputs:
- purified: float32 [4096, 4096], P('row', 'col')
- traces: float32 [2], replicated
Inputs may be any that keep to these rules, and one draw needn't show every extreme that they name: `pattern`: symmetric; every diagonal block is 1. `density`: symmetric, and zero in every block where pattern is 0. `step_choices`: one step squares and the other takes 2X - X^2.
All inputs are finite; a program needn't handle non-finite values.
Results may differ from a plain program's by a relative error of at most 0.0003.
Values sent between devices are 32-bit elements; how exact they have to be, the bound alone decides.
A program may use at most 64 MiB of HBM per device.

v0:
```python
import jax
import jax.numpy as jnp
from jax import lax
from jax.sharding import PartitionSpec as P

B = 128
STEPS = 2


def square_product(density):
    row_range = lax.all_gather(density, "col", axis=1, tiled=True)
    return jnp.dot(
        row_range,
        lax.all_gather(density, "row", axis=0, tiled=True),
        precision=lax.Precision.HIGHEST,
        preferred_element_type=jnp.float32,
    )


def shards(density, pattern, step_choices):
    row_height, col_width = density.shape
    element_mask = jnp.repeat(jnp.repeat(pattern, B, 0), B, 1).astype(jnp.float32)
    row_start = lax.axis_index("row") * row_height
    col_start = lax.axis_index("col") * col_width
    row_ids = row_start + jnp.arange(row_height, dtype=jnp.int32)[:, None]
    col_ids = col_start + jnp.arange(col_width, dtype=jnp.int32)[None, :]
    diagonal = (row_ids == col_ids).astype(jnp.float32)
    traces = []
    for section_index in range(STEPS):
        product = square_product(density)
        weight = step_choices[section_index].astype(jnp.float32)
        density = element_mask * ((1.0 - 2.0 * weight) * product + 2.0 * weight * density)
        local_trace = jnp.sum(density * diagonal)
        traces.append(lax.psum(local_trace, ("row", "col")))
    stacked = jnp.stack(traces)
    return (density, stacked)


def solution(mesh):
    return jax.shard_map(
        shards,
        mesh=mesh,
        in_specs=(P("row", "col"), P("row", "col"), P()),
        out_specs=(P("row", "col"), P()),
        check_vma=False,
    )
```

profile of v0, /device:TPU:1, one launch (start us, length us, event | category | flops | bytes accessed | tf_op | source)
XLA Modules:
  0.0 425.9 jit_solution(13444410139410536690)
XLA Ops:
  7.2 0.0 all-gather.5.cloned.1.call-start
  7.2 0.7 all-gather.5.cloned.1.call-update
  7.9 0.0 all-gather.7.cloned.1.call-start
  7.9 0.7 all-gather.7.cloned.1.call-update
  8.6 0.0 all-gather.9.cloned.1.call-start
  8.7 1.3 fusion.6
  10.7 0.7 convert_bitcast_fusion
  11.3 0.1 broadcast_bitcast_fusion
  11.4 73.3 %all-gather.5.cloned.1.call-done = f32[128,4096]{1,0:T(8,128)} async-done(((f32[128,256]{1,0:T(8,128)}), f32[128,4096]{1,0:T(8,128)}) %all-gather.5.cloned.1.call-update) | async-done | bytes 2097168 | tf_op jit(solution)/shard_map/all_gather | solution.py:11
  84.7 77.9 %all-gather.7.cloned.1.call-done = f32[4096,256]{1,0:T(8,128)} async-done(((f32[128,256]{1,0:T(8,128)}), f32[4096,256]{1,0:T(8,128)}) %all-gather.7.cloned.1.call-update) | async-done | bytes 4194320 | tf_op jit(solution)/shard_map/all_gather | solution.py:14
  162.6 5.6 %fusion.3 = f32[128,256]{1,0:T(8,128)} fusion(f32[128,4096]{1,0:T(8,128)} %all-gather.5.cloned.1.call-done, f32[4096,256]{1,0:T(8,128)} %all-gather.7.cloned.1.call-done, f32[128,256]{1,0:T(8,128)} %param.3, f32[]{:T(128)} %bitcast.3, f32[]{:T(128)S(6)} %sub.7, f32[256]{0:T(256)S(1)} %broadcast_bitcast_fusion), kind=kOutput, calls=%fused_computation.5 | convolution fusion | flops 1610743808 | bytes 6554632 | tf_op jit(solution)/shard_map/dot_general | solution.py:12
  168.3 0.0 all-gather.9.cloned.1.call-update
  168.3 0.0 all-gather.11.cloned.1.call-start
  168.3 0.5 all-gather.11.cloned.1.call-update
  169.5 65.5 %all-gather.9.cloned.1.call-done = f32[128,4096]{1,0:T(8,128)} async-done(((f32[128,256]{1,0:T(8,128)}), f32[128,4096]{1,0:T(8,128)}) %all-gather.9.cloned.1.call-update) | async-done | bytes 2097168 | tf_op jit(solution)/shard_map/all_gather | solution.py:11
  235.1 78.3 %all-gather.11.cloned.1.call-done = f32[4096,256]{1,0:T(8,128)} async-done(((f32[128,256]{1,0:T(8,128)}), f32[4096,256]{1,0:T(8,128)}) %all-gather.11.cloned.1.call-update) | async-done | bytes 4194320 | tf_op jit(solution)/shard_map/all_gather | solution.py:14
  313.4 6.2 %fusion.4 = (f32[]{:T(128)}, f32[]{:T(128)}, f32[128,256]{1,0:T(8,128)}) fusion(f32[128,256]{1,0:T(8,128)} %fusion.3, s32[256]{0:T(256)S(1)} %iota_add_fusion, s32[128]{0:T(128)S(1)} %iota_add_fusion.1, f32[]{:T(128)} %bitcast.2, f32[128,4096]{1,0:T(8,128)} %all-gather.9.cloned.1.call-done, f32[4096,256]{1,0:T(8,128)} %all-gather.11.cloned.1.call-done, ...), kind=kOutput, calls=%fused_computation.8 | convolution fusion | flops 1610907648 | bytes 6556176 | tf_op jit(solution)/shard_map/dot_general | solution.py:12
  319.7 97.9 %all-reduce = (f32[1]{0:T(128)}, f32[1]{0:T(128)}) all-reduce(f32[1]{0:T(128)} %bitcast.5, f32[1]{0:T(128)} %bitcast.4), channel_id=1, replica_groups=mesh['row'=32,'col'=16] {'row','col'}, use_global_device_ids=true, to_apply=%region_3.0 | all-reduce | flops 2 | bytes 16 | tf_op jit(solution)/shard_map/psum | solution.py:34
  417.6 1.8 pad_maximum_fusion
  (2 shorter events, 0.0 us)
Async XLA Ops:
  7.2 77.5 %all-gather.5.cloned.1.call-start = ((), (), s32[]{:S(2)}) async-start(), calls=%async_computation | async-start | bytes 2228224 | tf_op jit(solution)/shard_map/all_gather | solution.py:11
  7.9 154.7 %all-gather.7.cloned.1.call-start = ((), (), s32[]{:S(2)}) async-start(), calls=%async_computation.1 | async-start | bytes 4325376 | tf_op jit(solution)/shard_map/all_gather | solution.py:14
  8.6 226.4 %all-gather.9.cloned.1.call-start = ((), (), s32[]{:S(2)}) async-start(), calls=%async_computation.2 | async-start | bytes 2228224 | tf_op jit(solution)/shard_map/all_gather | solution.py:11
  168.3 145.2 %all-gather.11.cloned.1.call-start = ((), (), s32[]{:S(2)}) async-start(), calls=%async_computation.3 | async-start | bytes 4325376 | tf_op jit(solution)/shard_map/all_gather | solution.py:14
Sparse Core Ops, SparseCore 0:
  10.1 74.6 all-gather.4
  87.8 74.7 all-gather.6
  168.4 66.6 all-gather.8
  238.6 74.7 all-gather.10
where the time goes:
time: 426 us
  waiting for transfers between devices  297 us (70%)
  blocking collectives  97.9 us (23%)
  between operations  15.1 us (4%)
  matrix products  11.9 us (3%)
    all_gather x2, waiting for transfers between devices, square_product(): lax.all_gather(density, 'row', axis=0, tiled=True)  156 us
    all_gather x2, waiting for transfers between devices, square_product(): row_range = lax.all_gather(density, 'col', axis=1, tiled=True)  139 us
    psum x1, blocking collectives, shards(): traces.append(lax.psum(local_trace, ('row', 'col')))  97.9 us
    dot_general x2, matrix products, square_product(): jnp.dot(row_range, lax.all_gather(density, 'row', axis=0, tiled=True), pr...  11.9 us
  transfers between devices with their start and end apart: 4, of which 4 were waited for; matrix products, arithmetic and copies ran while one was open for 0% of the time, Pallas kernels for 0%

commit v1 on v0

v1 whole, which is shorter than its diff:
```python
import heapq

import jax
import jax.numpy as jnp
from jax import lax
from jax.experimental import pallas as pl
from jax.experimental.pallas import tpu as pltpu
from jax.sharding import PartitionSpec as P

B = 128
STEPS = 2
NZ, NL, NH, NX = 8, 2, 4, 4
NK = NZ * NL
NP = 2
CROSS = (0, 2, 6)
MESH = pl.DeviceIdType.MESH
F32 = jnp.float32


def row_route(d, s, p):
    low = p < NP // 2
    go = []
    if s == 0:
        if d == 0:
            go += ["zp", "zm"]
        elif d in (1, 2) or (d == 3 and low):
            go += ["zp"]
        elif d in (7, 6) or (d == 5 and not low):
            go += ["zm"]
        if d in CROSS:
            go += ["yc"]
    else:
        if d == 0:
            go += ["zp", "zm"]
        else:
            nxt, prv = (d + 1) % NZ, (d - 1) % NZ
            if d < 4 and nxt not in CROSS and (d < 3 or low):
                go += ["zp"]
            if d > 4 and prv not in CROSS and (d > 5 or not low):
                go += ["zm"]
    return go


def col_route(e, g, p):
    low = p < NP // 2
    go = []
    if g == 0:
        if e == 0:
            go += ["yp", "ym"]
        elif e == 1 and low:
            go += ["yp"]
        elif e == 3 and not low:
            go += ["ym"]
        go += ["xp", "xm"]
    elif g == 1 and low:
        go += ["xp"]
    elif g == 3 and not low:
        go += ["xm"]
    return go


def landing(kind, i, j, way):
    if kind == "a":
        if way == "yc":
            return i, 1 - j
        return ((i + (1 if way == "zp" else -1)) % NZ, j)
    if way[0] == "y":
        return ((i + (1 if way == "yp" else -1)) % NH, j)
    return (i, (j + (1 if way == "xp" else -1)) % NX)


def arrival_order():
    wire = 2.8 / NP
    cost = {"zp": wire, "zm": wire, "yc": wire, "xp": wire, "xm": wire, "yp": 2 * wire, "ym": 2 * wire}
    lag = {"zp": 1.7, "zm": 1.7, "yc": 1.7, "xp": 1.7, "xm": 1.7, "yp": 2.4, "ym": 2.4}
    free = dict.fromkeys(cost, 0.0)
    ready, order, tick = [], [], 0
    for p in range(NP):
        heapq.heappush(ready, (0.0, tick, ("b", 0, 0, p)))
        heapq.heappush(ready, (1.0 * (p >= NP // 2), tick + 1, ("a", 0, 0, p)))
        tick += 2
    while ready:
        now, _, (kind, i, j, p) = heapq.heappop(ready)
        if (i, j) != (0, 0):
            order.append((kind, i, j, p))
        for way in (row_route if kind == "a" else col_route)(i, j, p):
            start = max(now, free[way])
            free[way] = start + cost[way]
            ii, jj = landing(kind, i, j, way)
            heapq.heappush(ready, (free[way] + lag[way], tick, (kind, ii, jj, p)))
            tick += 1
    return order


ORDER = arrival_order()
assert len(ORDER) == len(set(ORDER)) == 2 * (NK - 1) * NP
NSEND = 160


def split(v):
    hi = v.astype(jnp.bfloat16)
    return hi, (v - hi.astype(F32)).astype(jnp.bfloat16)


def fold(v):
    return jnp.sum(v.reshape(-1, 8, 2, 128), axis=(0, 2))


def kernel(choice_ref, pat_ref, x_ref, out_ref, tr_ref, abuf, bbuf, part, gift, sums, got,
           asem, bsem, swap_sem, gift_sem, tr_sem, send_sem, tr_send):
    row, col = lax.axis_index("row"), lax.axis_index("col")
    core, x, yh = row % 2, (row // 2) % NX, row // (2 * NX)
    yl, z = col % NL, col // NL

    def at(core_=None, x_=None, yh_=None, yl_=None, z_=None):
        c = core if core_ is None else core_
        xx = x if x_ is None else x_
        h = yh if yh_ is None else yh_
        l = yl if yl_ is None else yl_
        zz = z if z_ is None else z_
        return ((h * NX + xx) * 2 + c, zz * NL + l)

    near = {
        "zp": at(z_=(z + 1) % NZ),
        "zm": at(z_=(z + NZ - 1) % NZ),
        "yc": at(yl_=1 - yl),
        "yp": at(yh_=(yh + 1) % NH),
        "ym": at(yh_=(yh + NH - 1) % NH),
        "xp": at(x_=(x + 1) % NX),
        "xm": at(x_=(x + NX - 1) % NX),
        "c": at(core_=1 - core),
    }
    barrier = pltpu.get_barrier_semaphore()
    for place in near.values():
        pl.semaphore_signal(barrier, inc=1, device_id=place, device_id_type=MESH)
    pl.semaphore_wait(barrier, len(near))

    def akey(d, s):
        return ((z + NZ - d) % NZ) * NL + (yl if s == 0 else 1 - yl)

    def bkey(e, g):
        return ((yh + NH - e) % NH) * NX + (x + NX - g) % NX

    AR, BR = 2 * B // NP, B // NP

    def place(kind, step, i, j, p):
        if kind == "a":
            return abuf.at[step, akey(i, j), pl.ds(p * AR, AR), :]
        return bbuf.at[step, bkey(i, j), pl.ds(p * BR, BR), :]

    def sem_of(kind, step, i, j, p):
        return asem.at[step, i, j, p] if kind == "a" else bsem.at[step, i, j, p]

    pending = []

    def send(src, dst, step, recv_sem, where):
        copy = pltpu.make_async_remote_copy(
            src_ref=src, dst_ref=dst, send_sem=send_sem.at[step, len(pending)], recv_sem=recv_sem,
            device_id=where, device_id_type=MESH)
        copy.start()
        pending.append(copy)

    def arrive(ref, sem, step):
        pltpu.make_async_remote_copy(
            src_ref=ref, dst_ref=ref, send_sem=send_sem.at[step, NSEND - 1], recv_sem=sem,
            device_id=near["c"], device_id_type=MESH).wait_recv()

    def forward(kind, step, i, j, p, p_route, src=None):
        here = place(kind, step, i, j, p)
        for way in (row_route if kind == "a" else col_route)(i, j, p_route):
            ii, jj = landing(kind, i, j, way)
            send(here if src is None else src, here, step, sem_of(kind, step, ii, jj, p), near[way])

    mine = pl.ds(core * B, B)
    theirs = pl.ds((1 - core) * B, B)
    off = row * B - col * 2 * B
    diag = (lax.broadcasted_iota(jnp.int32, (B, 2 * B), 0) + off
            == lax.broadcasted_iota(jnp.int32, (B, 2 * B), 1)).astype(F32)
    mask = [pat_ref[0, h].astype(F32) for h in range(2)]

    groups = [
        [at(z_=(z + i) % NZ) for i in range(1, NZ)],
        [at(x_=(x + i) % NX) for i in range(1, NX)],
        [at(yh_=(yh + i) % NH) for i in range(1, NH)],
        [at(yl_=1 - yl)],
        [at(core_=1 - core)],
    ]
    tr_copies = []

    def tr_start(stage):
        for n, where in enumerate(groups[stage]):
            copy = pltpu.make_async_remote_copy(
                src_ref=sums.at[stage], dst_ref=got.at[stage, n], send_sem=tr_send.at[stage, n],
                recv_sem=tr_sem.at[stage, n], device_id=where, device_id_type=MESH)
            copy.start()
            tr_copies.append((stage, copy))

    def tr_finish(stage):
        total = sums[stage]
        for n, (_, copy) in enumerate([c for c in tr_copies if c[0] == stage]):
            copy.wait_recv()
            total = total + got[stage, n]
        sums[stage + 1] = total

    for step in range(STEPS):
        own_b = bbuf.at[step, bkey(0, 0)]
        tile = x_ref if step == 0 else own_b
        send(tile.at[:, theirs], abuf.at[step, akey(0, 0), mine, :], step, swap_sem.at[step], near["c"])
        for p in range(NP):
            forward("b", step, 0, 0, p, p, tile.at[pl.ds(p * BR, BR), :])
        now = tile[...]
        if step == 0:
            own_b[...] = now
        abuf[step, akey(0, 0), mine, :] = tile[:, mine]
        for p in range(NP // 2):
            forward("a", step, 0, 0, core * (NP // 2) + p, 0)
        arrive(abuf.at[step, akey(0, 0), theirs, :], swap_sem.at[step], step)
        for p in range(NP // 2):
            forward("a", step, 0, 0, (1 - core) * (NP // 2) + p, 0)
        sums[0, 2 * step] = fold(now * now)
        sums[0, 2 * step + 1] = fold(now * diag)
        if step == 1:
            tr_start(0)
        stage_at = {len(ORDER) * (n + 3) // 8: n for n in range(5)}
        for n, (kind, i, j, p) in enumerate(ORDER):
            arrive(place(kind, step, i, j, p), sem_of(kind, step, i, j, p), step)
            forward(kind, step, i, j, p, p)
            if step == 1 and n in stage_at:
                tr_finish(stage_at[n])
                if stage_at[n] < 4:
                    tr_start(stage_at[n] + 1)
        acc = jnp.zeros((2 * B, 2 * B), F32)
        for k in range(NK // 2):
            a = jnp.concatenate([abuf[step, 2 * k], abuf[step, 2 * k + 1]], axis=1)
            b = jnp.concatenate([bbuf[step, 2 * k], bbuf[step, 2 * k + 1]], axis=0)
            ah, al = split(a)
            bh, bl = split(b)
            acc += (jnp.dot(ah, bh, preferred_element_type=F32) + jnp.dot(al, bh, preferred_element_type=F32)
                    + jnp.dot(ah, bl, preferred_element_type=F32))
        part[step] = acc
        send(part.at[step, theirs, :], gift.at[step], step, gift_sem.at[step], near["c"])
        arrive(gift.at[step], gift_sem.at[step], step)
        product = part[step, mine, :] + gift[step]
        w = choice_ref[step].astype(F32)
        for h in range(2):
            lanes = slice(h * B, (h + 1) * B)
            new = mask[h] * ((1.0 - 2.0 * w) * product[:, lanes] + 2.0 * w * now[:, lanes])
            if step == STEPS - 1:
                out_ref[:, lanes] = new
            else:
                bbuf[step + 1, bkey(0, 0), :, lanes] = new
        for copy in pending:
            copy.wait_send()
        pending.clear()
    for _, copy in tr_copies:
        copy.wait_send()
    for step in range(STEPS):
        w = choice_ref[step].astype(F32)
        square, plain = jnp.sum(sums[5, 2 * step]), jnp.sum(sums[5, 2 * step + 1])
        tr_ref[step] = (1.0 - 2.0 * w) * square + 2.0 * w * plain


def shards(density, pattern, step_choices):
    vmem, smem = (pl.BlockSpec(memory_space=m) for m in (pltpu.VMEM, pltpu.SMEM))
    dma = pltpu.SemaphoreType.DMA
    return pl.pallas_call(
        kernel,
        out_shape=(jax.ShapeDtypeStruct(density.shape, F32), jax.ShapeDtypeStruct((STEPS,), F32)),
        in_specs=[smem, smem, vmem],
        out_specs=(vmem, smem),
        scratch_shapes=[
            pltpu.VMEM((STEPS, NK, 2 * B, B), F32),
            pltpu.VMEM((STEPS, NK, B, 2 * B), F32),
            pltpu.VMEM((STEPS, 2 * B, 2 * B), F32),
            pltpu.VMEM((STEPS, B, 2 * B), F32),
            pltpu.VMEM((6, 2 * STEPS, 8, 128), F32),
            pltpu.VMEM((5, 7, 2 * STEPS, 8, 128), F32),
            dma((STEPS, NZ, NL, NP)),
            dma((STEPS, NH, NX, NP)),
            dma((STEPS,)),
            dma((STEPS,)),
            dma((5, 7)),
            dma((STEPS, NSEND)),
            dma((5, 7)),
        ],
        compiler_params=pltpu.CompilerParams(collective_id=0, has_side_effects=True),
    )(step_choices, pattern, density)


def solution(mesh):
    return jax.shard_map(
        shards,
        mesh=mesh,
        in_specs=(P("row", "col"), P("row", "col"), P()),
        out_specs=(P("row", "col"), P()),
        check_vma=False,
    )
```

time: 426 us -> 90.8 us (0.21)
  waiting for transfers between devices: 297 us -> 0 us
  blocking collectives: 97.9 us -> 0 us
  Pallas kernels: 0 us -> 87.9 us
  between operations: 15.1 us -> 0.65 us
  matrix products: 11.9 us -> 0 us
    all_gather x4 -> x0, waiting for transfers between devices: 295 us -> none  [the longest x2 156 us: square_product(): lax.all_gather(density, 'row', axis=0, tiled=True)]
    psum x1 -> x0, blocking collectives: 97.9 us -> none  [shards(): traces.append(lax.psum(local_trace, ('row', 'col')))]
    pallas_call x0 -> x1, Pallas kernels: none -> 87.9 us  [shards(): pl.pallas_call(kernel, out_shape=(jax.ShapeDtypeStruct(density.shape, F32...]
    dot_general x2 -> x0, matrix products: 11.9 us -> none  [square_product(): jnp.dot(row_range, lax.all_gather(density, 'row', axis=0, tiled=True), pr...]
  transfers between devices with their start and end apart: 4 -> 0, of which waited for: 4 -> 0; matrix products, arithmetic and copies ran while one was open for 0% -> 0% of each run, Pallas kernels for 0% -> 0%
where the time goes in v1:
time: 90.8 us; the launch traced here: 90.6 us
  Pallas kernels  87.9 us (97%)
  local copies, waits for them, and re-layouts  2.08 us (2%)
    pallas_call x1, Pallas kernels, shards(): pl.pallas_call(kernel, out_shape=(jax.ShapeDtypeStruct(density.shape, F32...  87.9 us
    unnamed x4, local copies, waits for them, and re-layouts  2.08 us

profile of v1, /device:TPU:1, one launch (start us, length us, event | category | flops | bytes accessed | tf_op | source)
XLA Modules:
  0.0 90.6 jit_solution(12280292328833587110)
XLA Ops:
  0.6 87.9 %shard_map.50 = (f32[128,256]{1,0:T(8,128)}, f32[2]{0:T(128)}) custom-call(s32[2]{0:T(128)} %choice_ref.1, s32[1,2]{1,0:T(1,128)} %pat_ref.1, f32[128,256]{1,0:T(8,128)} %x_ref.1), custom_call_target="tpu_custom_call" | custom-call | tf_op jit(solution)/shard_map/pallas_call | solution.py:266
  88.5 0.0 copy-start
  88.5 1.6 %copy.7 = f32[128,256]{1,0:T(8,128)} copy(f32[128,256]{1,0:T(8,128)} %get-tuple-element.4) | data formatting | bytes 262144
  90.1 0.0 copy-done
  90.1 0.5 copy.8
Async XLA Ops:
  88.5 1.6 %copy-start = (f32[2]{0:T(128)S(1)}, f32[2]{0:T(128)}, u32[]{:S(2)}) copy-start(f32[2]{0:T(128)} %get-tuple-element.5) | copy-start | bytes 28

commit v2 on v1

--- a/solution.py
+++ b/solution.py
@@ -1,5 +1,3 @@
-import heapq
-
 import jax
 import jax.numpy as jnp
 from jax import lax
@@ -12,7 +10,7 @@
 NZ, NL, NH, NX = 8, 2, 4, 4
 NK = NZ * NL
 NP = 2
-CROSS = (0, 2, 6)
+CROSS = (0, 3, 5)
 MESH = pl.DeviceIdType.MESH
 F32 = jnp.float32
 
@@ -69,32 +67,21 @@
     return (i, (j + (1 if way == "xp" else -1)) % NX)
 
 
-def arrival_order():
-    wire = 2.8 / NP
-    cost = {"zp": wire, "zm": wire, "yc": wire, "xp": wire, "xm": wire, "yp": 2 * wire, "ym": 2 * wire}
-    lag = {"zp": 1.7, "zm": 1.7, "yc": 1.7, "xp": 1.7, "xm": 1.7, "yp": 2.4, "ym": 2.4}
-    free = dict.fromkeys(cost, 0.0)
-    ready, order, tick = [], [], 0
-    for p in range(NP):
-        heapq.heappush(ready, (0.0, tick, ("b", 0, 0, p)))
-        heapq.heappush(ready, (1.0 * (p >= NP // 2), tick + 1, ("a", 0, 0, p)))
-        tick += 2
-    while ready:
-        now, _, (kind, i, j, p) = heapq.heappop(ready)
-        if (i, j) != (0, 0):
-            order.append((kind, i, j, p))
-        for way in (row_route if kind == "a" else col_route)(i, j, p):
-            start = max(now, free[way])
-            free[way] = start + cost[way]
-            ii, jj = landing(kind, i, j, way)
-            heapq.heappush(ready, (free[way] + lag[way], tick, (kind, ii, jj, p)))
-            tick += 1
-    return order
-
-
-ORDER = arrival_order()
+ORDER = [
+    ("b", 0, 3, 0), ("a", 7, 0, 0), ("a", 1, 0, 0), ("b", 0, 1, 0), ("a", 7, 0, 1), ("b", 1, 0, 0),
+    ("a", 1, 0, 1), ("b", 3, 0, 0), ("a", 2, 0, 0), ("b", 3, 0, 1), ("b", 1, 0, 1), ("a", 6, 0, 0),
+    ("b", 0, 1, 1), ("a", 6, 0, 1), ("a", 2, 0, 1), ("a", 0, 1, 0), ("a", 0, 1, 1), ("b", 1, 1, 0),
+    ("b", 0, 3, 1), ("a", 3, 0, 0), ("b", 3, 1, 0), ("b", 1, 3, 0), ("b", 2, 0, 0), ("a", 5, 0, 1),
+    ("b", 2, 0, 1), ("b", 3, 3, 1), ("a", 5, 0, 0), ("a", 3, 0, 1), ("b", 1, 3, 1), ("a", 7, 1, 0),
+    ("a", 1, 1, 0), ("b", 3, 3, 0), ("a", 3, 1, 0), ("a", 7, 1, 1), ("b", 1, 2, 0), ("b", 3, 2, 0),
+    ("a", 1, 1, 1), ("b", 3, 1, 1), ("a", 5, 1, 1), ("b", 2, 1, 0), ("a", 4, 0, 0), ("b", 2, 3, 0),
+    ("b", 0, 2, 1), ("b", 2, 3, 1), ("a", 6, 1, 0), ("a", 2, 1, 0), ("a", 4, 0, 1), ("b", 1, 1, 1),
+    ("a", 6, 1, 1), ("a", 5, 1, 0), ("a", 3, 1, 1), ("a", 4, 1, 0), ("a", 2, 1, 1), ("b", 1, 2, 1),
+    ("a", 4, 1, 1), ("b", 2, 1, 1), ("b", 0, 2, 0), ("b", 2, 2, 0), ("b", 3, 2, 1), ("b", 2, 2, 1),
+]
 assert len(ORDER) == len(set(ORDER)) == 2 * (NK - 1) * NP
-NSEND = 160
+STAGE_AT = {9: 0, 29: 1, 54: 2}
+NSEND = 80 * NP
 
 
 def split(v):
@@ -103,11 +90,12 @@
 
 
 def fold(v):
-    return jnp.sum(v.reshape(-1, 8, 2, 128), axis=(0, 2))
+    rows = jnp.sum(v, axis=0, keepdims=True)
+    return rows[:, :128] + rows[:, 128:]
 
 
 def kernel(choice_ref, pat_ref, x_ref, out_ref, tr_ref, abuf, bbuf, part, gift, sums, got,
-           asem, bsem, swap_sem, gift_sem, tr_sem, send_sem, tr_send):
+           asem, bsem, swap_sem, gift_sem, tr_sem, send_sem, tr_send, fetch_sem):
     row, col = lax.axis_index("row"), lax.axis_index("col")
     core, x, yh = row % 2, (row // 2) % NX, row // (2 * NX)
     yl, z = col % NL, col // NL
@@ -130,16 +118,26 @@
         "xm": at(x_=(x + NX - 1) % NX),
         "c": at(core_=1 - core),
     }
-    barrier = pltpu.get_barrier_semaphore()
-    for place in near.values():
-        pl.semaphore_signal(barrier, inc=1, device_id=place, device_id_type=MESH)
-    pl.semaphore_wait(barrier, len(near))
-
+    near_other = {
+        "zp": at(core_=1 - core, z_=(z + 1) % NZ),
+        "zm": at(core_=1 - core, z_=(z + NZ - 1) % NZ),
+        "yc": at(core_=1 - core, yl_=1 - yl),
+    }
     def akey(d, s):
         return ((z + NZ - d) % NZ) * NL + (yl if s == 0 else 1 - yl)
 
     def bkey(e, g):
         return ((yh + NH - e) % NH) * NX + (x + NX - g) % NX
+
+    barrier = pltpu.get_barrier_semaphore()
+    greeted = [*near.values(), *near_other.values()]
+    for place in greeted:
+        pl.semaphore_signal(barrier, inc=1, device_id=place, device_id_type=MESH)
+    sums[0] = jnp.zeros((8, 128), F32)
+    fetch = pltpu.make_async_copy(x_ref, bbuf.at[0, bkey(0, 0)], fetch_sem)
+    fetch.start()
+    pl.semaphore_wait(barrier, len(greeted))
+    fetch.wait()
 
     AR, BR = 2 * B // NP, B // NP
 
@@ -165,11 +163,11 @@
             src_ref=ref, dst_ref=ref, send_sem=send_sem.at[step, NSEND - 1], recv_sem=sem,
             device_id=near["c"], device_id_type=MESH).wait_recv()
 
-    def forward(kind, step, i, j, p, p_route, src=None):
+    def forward(kind, step, i, j, p, p_route):
         here = place(kind, step, i, j, p)
         for way in (row_route if kind == "a" else col_route)(i, j, p_route):
             ii, jj = landing(kind, i, j, way)
-            send(here if src is None else src, here, step, sem_of(kind, step, ii, jj, p), near[way])
+            send(here, here, step, sem_of(kind, step, ii, jj, p), near[way])
 
     mine = pl.ds(core * B, B)
     theirs = pl.ds((1 - core) * B, B)
@@ -180,10 +178,9 @@
 
     groups = [
         [at(z_=(z + i) % NZ) for i in range(1, NZ)],
-        [at(x_=(x + i) % NX) for i in range(1, NX)],
+        [at(x_=(x + i) % NX, yl_=(yl + j) % NL) for i in range(NX) for j in range(NL) if i or j],
         [at(yh_=(yh + i) % NH) for i in range(1, NH)],
-        [at(yl_=1 - yl)],
-        [at(core_=1 - core)],
+        [near["c"]],
     ]
     tr_copies = []
 
@@ -203,32 +200,30 @@
         sums[stage + 1] = total
 
     for step in range(STEPS):
-        own_b = bbuf.at[step, bkey(0, 0)]
-        tile = x_ref if step == 0 else own_b
-        send(tile.at[:, theirs], abuf.at[step, akey(0, 0), mine, :], step, swap_sem.at[step], near["c"])
-        for p in range(NP):
-            forward("b", step, 0, 0, p, p, tile.at[pl.ds(p * BR, BR), :])
+        tile = bbuf.at[step, bkey(0, 0)]
+        own_a = abuf.at[step, akey(0, 0), mine, :]
+        for n in range(3):
+            if n < 2:
+                for way in row_route(0, 0, 0)[2 * n: 2 * n + 2]:
+                    landed = asem.at[step, *landing("a", 0, 0, way), core]
+                    send(tile.at[:, mine], own_a, step, landed, near[way])
+                    send(tile.at[:, theirs], own_a, step, landed, near_other[way])
+            if n > 0:
+                forward("b", step, 0, 0, n - 1, n - 1)
+        send(tile.at[:, theirs], own_a, step, swap_sem.at[step], near["c"])
         now = tile[...]
-        if step == 0:
-            own_b[...] = now
         abuf[step, akey(0, 0), mine, :] = tile[:, mine]
-        for p in range(NP // 2):
-            forward("a", step, 0, 0, core * (NP // 2) + p, 0)
-        arrive(abuf.at[step, akey(0, 0), theirs, :], swap_sem.at[step], step)
-        for p in range(NP // 2):
-            forward("a", step, 0, 0, (1 - core) * (NP // 2) + p, 0)
-        sums[0, 2 * step] = fold(now * now)
-        sums[0, 2 * step + 1] = fold(now * diag)
+        sums[0, 2 * step: 2 * step + 1] = fold(now * now)
+        sums[0, 2 * step + 1: 2 * step + 2] = fold(now * diag)
         if step == 1:
             tr_start(0)
-        stage_at = {len(ORDER) * (n + 3) // 8: n for n in range(5)}
         for n, (kind, i, j, p) in enumerate(ORDER):
             arrive(place(kind, step, i, j, p), sem_of(kind, step, i, j, p), step)
             forward(kind, step, i, j, p, p)
-            if step == 1 and n in stage_at:
-                tr_finish(stage_at[n])
-                if stage_at[n] < 4:
-                    tr_start(stage_at[n] + 1)
+            if step == 1 and n in STAGE_AT:
+                tr_finish(STAGE_AT[n])
+                tr_start(STAGE_AT[n] + 1)
+        arrive(abuf.at[step, akey(0, 0), theirs, :], swap_sem.at[step], step)
         acc = jnp.zeros((2 * B, 2 * B), F32)
         for k in range(NK // 2):
             a = jnp.concatenate([abuf[step, 2 * k], abuf[step, 2 * k + 1]], axis=1)
@@ -240,6 +235,8 @@
         part[step] = acc
         send(part.at[step, theirs, :], gift.at[step], step, gift_sem.at[step], near["c"])
         arrive(gift.at[step], gift_sem.at[step], step)
+        if step == 1:
+            tr_finish(3)
         product = part[step, mine, :] + gift[step]
         w = choice_ref[step].astype(F32)
         for h in range(2):
@@ -256,7 +253,7 @@
         copy.wait_send()
     for step in range(STEPS):
         w = choice_ref[step].astype(F32)
-        square, plain = jnp.sum(sums[5, 2 * step]), jnp.sum(sums[5, 2 * step + 1])
+        square, plain = jnp.sum(sums[4, 2 * step: 2 * step + 1]), jnp.sum(sums[4, 2 * step + 1: 2 * step + 2])
         tr_ref[step] = (1.0 - 2.0 * w) * square + 2.0 * w * plain
 
 
@@ -266,22 +263,23 @@
     return pl.pallas_call(
         kernel,
         out_shape=(jax.ShapeDtypeStruct(density.shape, F32), jax.ShapeDtypeStruct((STEPS,), F32)),
-        in_specs=[smem, smem, vmem],
+        in_specs=[smem, smem, pl.BlockSpec(memory_space=pl.ANY)],
         out_specs=(vmem, smem),
         scratch_shapes=[
             pltpu.VMEM((STEPS, NK, 2 * B, B), F32),
             pltpu.VMEM((STEPS, NK, B, 2 * B), F32),
             pltpu.VMEM((STEPS, 2 * B, 2 * B), F32),
             pltpu.VMEM((STEPS, B, 2 * B), F32),
-            pltpu.VMEM((6, 2 * STEPS, 8, 128), F32),
-            pltpu.VMEM((5, 7, 2 * STEPS, 8, 128), F32),
+            pltpu.VMEM((5, 8, 128), F32),
+            pltpu.VMEM((4, 7, 8, 128), F32),
             dma((STEPS, NZ, NL, NP)),
             dma((STEPS, NH, NX, NP)),
             dma((STEPS,)),
             dma((STEPS,)),
-            dma((5, 7)),
+            dma((4, 7)),
             dma((STEPS, NSEND)),
-            dma((5, 7)),
+            dma((4, 7)),
+            dma(()),
         ],
         compiler_params=pltpu.CompilerParams(collective_id=0, has_side_effects=True),
     )(step_choices, pattern, density)

time: 90.8 us -> 83.2 us (0.916)
  Pallas kernels: 87.9 us -> 80.3 us
    pallas_call x1, Pallas kernels: 87.9 us -> 80.3 us  [shards(): pl.pallas_call(kernel, out_shape=(jax.ShapeDtypeStruct(density.shape, F32...]
where the time goes in v2:
time: 83.2 us; the launch traced here: 83 us
  Pallas kernels  80.3 us (97%)
  local copies, waits for them, and re-layouts  2.08 us (2%)
    pallas_call x1, Pallas kernels, shards(): pl.pallas_call(kernel, out_shape=(jax.ShapeDtypeStruct(density.shape, F32...  80.3 us
    unnamed x4, local copies, waits for them, and re-layouts  2.08 us

profile of v2, /device:TPU:1, one launch (start us, length us, event | category | flops | bytes accessed | tf_op | source)
XLA Modules:
  0.0 83.0 jit_solution(2496226676869358259)
XLA Ops:
  0.6 80.3 %shard_map.50 = (f32[128,256]{1,0:T(8,128)}, f32[2]{0:T(128)}) custom-call(s32[2]{0:T(128)} %choice_ref.1, s32[1,2]{1,0:T(1,128)} %pat_ref.1, f32[128,256]{1,0:T(8,128)} %x_ref.1), custom_call_target="tpu_custom_call" | custom-call | tf_op jit(solution)/shard_map/pallas_call | solution.py:263
  80.9 0.0 copy-start
  80.9 1.6 %copy.7 = f32[128,256]{1,0:T(8,128)} copy(f32[128,256]{1,0:T(8,128)} %get-tuple-element.4) | data formatting | bytes 262144
  82.5 0.0 copy-done
  82.5 0.5 copy.8
Async XLA Ops:
  80.9 1.6 %copy-start = (f32[2]{0:T(128)S(1)}, f32[2]{0:T(128)}, u32[]{:S(2)}) copy-start(f32[2]{0:T(128)} %get-tuple-element.5) | copy-start | bytes 28

commit v3 on v2

--- a/solution.py
+++ b/solution.py
@@ -95,7 +95,7 @@
 
 
 def kernel(choice_ref, pat_ref, x_ref, out_ref, tr_ref, abuf, bbuf, part, gift, sums, got,
-           asem, bsem, swap_sem, gift_sem, tr_sem, send_sem, tr_send, fetch_sem):
+           asem, bsem, swap_sem, gift_sem, tr_sem, send_sem, tr_send, fetch_sem, half):
     row, col = lax.axis_index("row"), lax.axis_index("col")
     core, x, yh = row % 2, (row // 2) % NX, row // (2 * NX)
     yl, z = col % NL, col // NL
@@ -201,18 +201,20 @@
 
     for step in range(STEPS):
         tile = bbuf.at[step, bkey(0, 0)]
+        for p in range(NP):
+            forward("b", step, 0, 0, p, p)
         own_a = abuf.at[step, akey(0, 0), mine, :]
-        for n in range(3):
-            if n < 2:
-                for way in row_route(0, 0, 0)[2 * n: 2 * n + 2]:
-                    landed = asem.at[step, *landing("a", 0, 0, way), core]
-                    send(tile.at[:, mine], own_a, step, landed, near[way])
-                    send(tile.at[:, theirs], own_a, step, landed, near_other[way])
-            if n > 0:
-                forward("b", step, 0, 0, n - 1, n - 1)
-        send(tile.at[:, theirs], own_a, step, swap_sem.at[step], near["c"])
+        other = half.at[step]
+        abuf[step, akey(0, 0), mine, :] = tile[:, mine]
+        half[step] = tile[:, theirs]
+        for way in row_route(0, 0, 0):
+            landed = asem.at[step, *landing("a", 0, 0, way), core]
+            send(own_a, own_a, step, landed, near[way])
+        for way in row_route(0, 0, 0):
+            landed = asem.at[step, *landing("a", 0, 0, way), core]
+            send(other, own_a, step, landed, near_other[way])
+        send(other, own_a, step, swap_sem.at[step], near["c"])
         now = tile[...]
-        abuf[step, akey(0, 0), mine, :] = tile[:, mine]
         sums[0, 2 * step: 2 * step + 1] = fold(now * now)
         sums[0, 2 * step + 1: 2 * step + 2] = fold(now * diag)
         if step == 1:
@@ -280,6 +282,7 @@
             dma((STEPS, NSEND)),
             dma((4, 7)),
             dma(()),
+            pltpu.VMEM((STEPS, B, B), F32),
         ],
         compiler_params=pltpu.CompilerParams(collective_id=0, has_side_effects=True),
     )(step_choices, pattern, density)

time: 83.2 us -> 75.9 us (0.912)
  Pallas kernels: 80.3 us -> 73.1 us
    pallas_call x1, Pallas kernels: 80.3 us -> 73.1 us  [shards(): pl.pallas_call(kernel, out_shape=(jax.ShapeDtypeStruct(density.shape, F32...]
where the time goes in v3:
time: 75.9 us; the launch traced here: 75.8 us
  Pallas kernels  73.1 us (96%)
  local copies, waits for them, and re-layouts  2.08 us (3%)
    pallas_call x1, Pallas kernels, shards(): pl.pallas_call(kernel, out_shape=(jax.ShapeDtypeStruct(density.shape, F32...  73.1 us
    unnamed x4, local copies, waits for them, and re-layouts  2.08 us

profile of v3, /device:TPU:1, one launch (start us, length us, event | category | flops | bytes accessed | tf_op | source)
XLA Modules:
  0.0 75.8 jit_solution(11408580339513741222)
XLA Ops:
  0.6 73.1 %shard_map.50 = (f32[128,256]{1,0:T(8,128)}, f32[2]{0:T(128)}) custom-call(s32[2]{0:T(128)} %choice_ref.1, s32[1,2]{1,0:T(1,128)} %pat_ref.1, f32[128,256]{1,0:T(8,128)} %x_ref.1), custom_call_target="tpu_custom_call" | custom-call | tf_op jit(solution)/shard_map/pallas_call | solution.py:265
  73.7 0.0 copy-start
  73.7 1.6 %copy.7 = f32[128,256]{1,0:T(8,128)} copy(f32[128,256]{1,0:T(8,128)} %get-tuple-element.4) | data formatting | bytes 262144
  75.3 0.0 copy-done
  75.3 0.5 copy.8
Async XLA Ops:
  73.7 1.6 %copy-start = (f32[2]{0:T(128)S(1)}, f32[2]{0:T(128)}, u32[]{:S(2)}) copy-start(f32[2]{0:T(128)} %get-tuple-element.5) | copy-start | bytes 28

commit v4 on v3

--- a/solution.py
+++ b/solution.py
@@ -81,6 +81,7 @@
 ]
 assert len(ORDER) == len(set(ORDER)) == 2 * (NK - 1) * NP
 STAGE_AT = {9: 0, 29: 1, 54: 2}
+GAPS = {3: 4, 4: 1, 7: 3, 8: 1, 12: 4, 13: 1, 15: 2, 18: 3, 21: 3, 23: 2, 28: 5, 31: 3, 32: 1, 37: 5, 42: 5, 47: 5, 51: 4, 58: 7}
 NSEND = 80 * NP
 
 
@@ -94,8 +95,8 @@
     return rows[:, :128] + rows[:, 128:]
 
 
-def kernel(choice_ref, pat_ref, x_ref, out_ref, tr_ref, abuf, bbuf, part, gift, sums, got,
-           asem, bsem, swap_sem, gift_sem, tr_sem, send_sem, tr_send, fetch_sem, half):
+def kernel(choice_hbm, pat_hbm, x_ref, out_ref, tr_ref, abuf, bbuf, part, gift, sums, got,
+           asem, bsem, swap_sem, gift_sem, tr_sem, send_sem, tr_send, fetch_sem, half, choice_ref, pat_ref, ahi, alo, bhi, blo):
     row, col = lax.axis_index("row"), lax.axis_index("col")
     core, x, yh = row % 2, (row // 2) % NX, row // (2 * NX)
     yl, z = col % NL, col // NL
@@ -134,8 +135,14 @@
     for place in greeted:
         pl.semaphore_signal(barrier, inc=1, device_id=place, device_id_type=MESH)
     sums[0] = jnp.zeros((8, 128), F32)
-    fetch = pltpu.make_async_copy(x_ref, bbuf.at[0, bkey(0, 0)], fetch_sem)
+    fetch = pltpu.make_async_copy(x_ref, bbuf.at[0, bkey(0, 0)], fetch_sem.at[0])
     fetch.start()
+    small = [
+        pltpu.make_async_copy(choice_hbm, choice_ref, fetch_sem.at[1]),
+        pltpu.make_async_copy(pat_hbm, pat_ref, fetch_sem.at[2]),
+    ]
+    for copy in small:
+        copy.start()
     pl.semaphore_wait(barrier, len(greeted))
     fetch.wait()
 
@@ -169,12 +176,16 @@
             ii, jj = landing(kind, i, j, way)
             send(here, here, step, sem_of(kind, step, ii, jj, p), near[way])
 
+    def halve(kind, step, i, j, rows):
+        key = akey(i, j) if kind == "a" else bkey(i, j)
+        whole, hi, lo = (abuf, ahi, alo) if kind == "a" else (bbuf, bhi, blo)
+        hi[key, rows, :], lo[key, rows, :] = split(whole[step, key, rows, :])
+
     mine = pl.ds(core * B, B)
     theirs = pl.ds((1 - core) * B, B)
     off = row * B - col * 2 * B
     diag = (lax.broadcasted_iota(jnp.int32, (B, 2 * B), 0) + off
             == lax.broadcasted_iota(jnp.int32, (B, 2 * B), 1)).astype(F32)
-    mask = [pat_ref[0, h].astype(F32) for h in range(2)]
 
     groups = [
         [at(z_=(z + i) % NZ) for i in range(1, NZ)],
@@ -182,24 +193,27 @@
         [at(yh_=(yh + i) % NH) for i in range(1, NH)],
         [near["c"]],
     ]
-    tr_copies = []
-
-    def tr_start(stage):
-        for n, where in enumerate(groups[stage]):
-            copy = pltpu.make_async_remote_copy(
+
+    def tr_copies(stage):
+        return [
+            pltpu.make_async_remote_copy(
                 src_ref=sums.at[stage], dst_ref=got.at[stage, n], send_sem=tr_send.at[stage, n],
                 recv_sem=tr_sem.at[stage, n], device_id=where, device_id_type=MESH)
+            for n, where in enumerate(groups[stage])
+        ]
+
+    def tr_start(stage):
+        for copy in tr_copies(stage):
             copy.start()
-            tr_copies.append((stage, copy))
 
     def tr_finish(stage):
         total = sums[stage]
-        for n, (_, copy) in enumerate([c for c in tr_copies if c[0] == stage]):
+        for n, copy in enumerate(tr_copies(stage)):
             copy.wait_recv()
             total = total + got[stage, n]
         sums[stage + 1] = total
 
-    for step in range(STEPS):
+    def advance(step, _):
         tile = bbuf.at[step, bkey(0, 0)]
         for p in range(NP):
             forward("b", step, 0, 0, p, p)
@@ -215,61 +229,92 @@
             send(other, own_a, step, landed, near_other[way])
         send(other, own_a, step, swap_sem.at[step], near["c"])
         now = tile[...]
-        sums[0, 2 * step: 2 * step + 1] = fold(now * now)
-        sums[0, 2 * step + 1: 2 * step + 2] = fold(now * diag)
-        if step == 1:
+        halve("b", step, 0, 0, pl.ds(0, B))
+        halve("a", step, 0, 0, mine)
+        sums[0, pl.ds(2 * step, 1)] = fold(now * now)
+        sums[0, pl.ds(2 * step + 1, 1)] = fold(now * diag)
+
+        @pl.when(step == STEPS - 1)
+        def _():
             tr_start(0)
+
+        waiting = []
         for n, (kind, i, j, p) in enumerate(ORDER):
             arrive(place(kind, step, i, j, p), sem_of(kind, step, i, j, p), step)
             forward(kind, step, i, j, p, p)
-            if step == 1 and n in STAGE_AT:
-                tr_finish(STAGE_AT[n])
-                tr_start(STAGE_AT[n] + 1)
+            waiting.append((kind, i, j, p))
+            for _ in range(len(waiting) if n + 1 == len(ORDER) else min(len(waiting), GAPS.get(n, 0))):
+                kind, i, j, p = waiting.pop(0)
+                halve(kind, step, i, j, pl.ds(p * AR, AR) if kind == "a" else pl.ds(p * BR, BR))
+            if n in STAGE_AT:
+                @pl.when(step == STEPS - 1)
+                def _():
+                    tr_finish(STAGE_AT[n])
+                    tr_start(STAGE_AT[n] + 1)
         arrive(abuf.at[step, akey(0, 0), theirs, :], swap_sem.at[step], step)
-        acc = jnp.zeros((2 * B, 2 * B), F32)
-        for k in range(NK // 2):
-            a = jnp.concatenate([abuf[step, 2 * k], abuf[step, 2 * k + 1]], axis=1)
-            b = jnp.concatenate([bbuf[step, 2 * k], bbuf[step, 2 * k + 1]], axis=0)
-            ah, al = split(a)
-            bh, bl = split(b)
-            acc += (jnp.dot(ah, bh, preferred_element_type=F32) + jnp.dot(al, bh, preferred_element_type=F32)
-                    + jnp.dot(ah, bl, preferred_element_type=F32))
-        part[step] = acc
+        halve("a", step, 0, 0, theirs)
+
+        def product_of(rows):
+            left_hi = jnp.concatenate([ahi[k, rows, :] for k in range(NK)], axis=1)
+            left_lo = jnp.concatenate([alo[k, rows, :] for k in range(NK)], axis=1)
+            right_hi = jnp.concatenate([bhi[k] for k in range(NK)], axis=0)
+            right_lo = jnp.concatenate([blo[k] for k in range(NK)], axis=0)
+            return (jnp.dot(left_hi, right_hi, preferred_element_type=F32)
+                    + jnp.dot(left_lo, right_hi, preferred_element_type=F32)
+                    + jnp.dot(left_hi, right_lo, preferred_element_type=F32))
+
+        part[step, theirs, :] = product_of(theirs)
         send(part.at[step, theirs, :], gift.at[step], step, gift_sem.at[step], near["c"])
+        part[step, mine, :] = product_of(mine)
+        for copy in pending[:-1]:
+            copy.wait_send()
         arrive(gift.at[step], gift_sem.at[step], step)
-        if step == 1:
+
+        @pl.when(step == STEPS - 1)
+        def _():
             tr_finish(3)
+
         product = part[step, mine, :] + gift[step]
+
+        @pl.when(step == 0)
+        def _():
+            for copy in small:
+                copy.wait()
+
+        mask = [pat_ref[0, h].astype(F32) for h in range(2)]
         w = choice_ref[step].astype(F32)
         for h in range(2):
             lanes = slice(h * B, (h + 1) * B)
             new = mask[h] * ((1.0 - 2.0 * w) * product[:, lanes] + 2.0 * w * now[:, lanes])
-            if step == STEPS - 1:
-                out_ref[:, lanes] = new
-            else:
-                bbuf[step + 1, bkey(0, 0), :, lanes] = new
-        for copy in pending:
+            bbuf[step + 1, bkey(0, 0), :, lanes] = new
+        pending[-1].wait_send()
+        pending.clear()
+        return 0
+
+    lax.fori_loop(0, STEPS, advance, 0)
+    store = pltpu.make_async_copy(bbuf.at[STEPS, bkey(0, 0)], out_ref, fetch_sem.at[0])
+    store.start()
+    for stage in range(len(groups)):
+        for copy in tr_copies(stage):
             copy.wait_send()
-        pending.clear()
-    for _, copy in tr_copies:
-        copy.wait_send()
     for step in range(STEPS):
         w = choice_ref[step].astype(F32)
         square, plain = jnp.sum(sums[4, 2 * step: 2 * step + 1]), jnp.sum(sums[4, 2 * step + 1: 2 * step + 2])
         tr_ref[step] = (1.0 - 2.0 * w) * square + 2.0 * w * plain
+    store.wait()
 
 
 def shards(density, pattern, step_choices):
-    vmem, smem = (pl.BlockSpec(memory_space=m) for m in (pltpu.VMEM, pltpu.SMEM))
+    smem = pl.BlockSpec(memory_space=pltpu.SMEM)
     dma = pltpu.SemaphoreType.DMA
     return pl.pallas_call(
         kernel,
         out_shape=(jax.ShapeDtypeStruct(density.shape, F32), jax.ShapeDtypeStruct((STEPS,), F32)),
-        in_specs=[smem, smem, pl.BlockSpec(memory_space=pl.ANY)],
-        out_specs=(vmem, smem),
+        in_specs=[pl.BlockSpec(memory_space=pltpu.HBM)] * 3,
+        out_specs=(pl.BlockSpec(memory_space=pl.ANY), smem),
         scratch_shapes=[
             pltpu.VMEM((STEPS, NK, 2 * B, B), F32),
-            pltpu.VMEM((STEPS, NK, B, 2 * B), F32),
+            pltpu.VMEM((STEPS + 1, NK, B, 2 * B), F32),
             pltpu.VMEM((STEPS, 2 * B, 2 * B), F32),
             pltpu.VMEM((STEPS, B, 2 * B), F32),
             pltpu.VMEM((5, 8, 128), F32),
@@ -281,8 +326,12 @@
             dma((4, 7)),
             dma((STEPS, NSEND)),
             dma((4, 7)),
-            dma(()),
+            dma((3,)),
             pltpu.VMEM((STEPS, B, B), F32),
+            pltpu.SMEM((STEPS,), jnp.int32),
+            pltpu.SMEM((1, 2), jnp.int32),
+            *[pltpu.VMEM((NK, 2 * B, B), jnp.bfloat16)] * 2,
+            *[pltpu.VMEM((NK, B, 2 * B), jnp.bfloat16)] * 2,
         ],
         compiler_params=pltpu.CompilerParams(collective_id=0, has_side_effects=True),
     )(step_choices, pattern, density)

time: 75.9 us -> 74 us (0.975)
  Pallas kernels: 73.1 us -> 71.2 us
    pallas_call x1, Pallas kernels: 73.1 us -> 71.2 us  [shards(): pl.pallas_call(kernel, out_shape=(jax.ShapeDtypeStruct(density.shape, F32...]
where the time goes in v4:
time: 74 us; the launch traced here: 73.9 us
  Pallas kernels  71.2 us (96%)
  local copies, waits for them, and re-layouts  2.08 us (3%)
    pallas_call x1, Pallas kernels, shards(): pl.pallas_call(kernel, out_shape=(jax.ShapeDtypeStruct(density.shape, F32...  71.2 us
    unnamed x4, local copies, waits for them, and re-layouts  2.08 us

profile of v4, /device:TPU:1, one launch (start us, length us, event | category | flops | bytes accessed | tf_op | source)
XLA Modules:
  0.0 73.9 jit_solution(16038472430444676805)
XLA Ops:
  0.6 71.2 %shard_map.50 = (f32[128,256]{1,0:T(8,128)}, f32[2]{0:T(128)}) custom-call(s32[2]{0:T(128)} %choice_hbm.1, s32[1,2]{1,0:T(1,128)} %pat_hbm.1, f32[128,256]{1,0:T(8,128)} %x_ref.1), custom_call_target="tpu_custom_call" | custom-call | tf_op jit(solution)/shard_map/pallas_call | solution.py:310
  71.8 0.0 copy-start
  71.8 1.6 %copy.7 = f32[128,256]{1,0:T(8,128)} copy(f32[128,256]{1,0:T(8,128)} %get-tuple-element.4) | data formatting | bytes 262144
  73.4 0.0 copy-done
  73.4 0.5 copy.8
Async XLA Ops:
  71.8 1.6 %copy-start = (f32[2]{0:T(128)S(1)}, f32[2]{0:T(128)}, u32[]{:S(2)}) copy-start(f32[2]{0:T(128)} %get-tuple-element.5) | copy-start | bytes 28

commit v5 on v4

--- a/solution.py
+++ b/solution.py
@@ -333,8 +333,8 @@
             *[pltpu.VMEM((NK, 2 * B, B), jnp.bfloat16)] * 2,
             *[pltpu.VMEM((NK, B, 2 * B), jnp.bfloat16)] * 2,
         ],
-        compiler_params=pltpu.CompilerParams(collective_id=0, has_side_effects=True),
-    )(step_choices, pattern, density)
+        compiler_params=pltpu.CompilerParams(collective_id=0, has_side_effects=True, vmem_limit_bytes=24 << 20),
+    )(*(pltpu.with_memory_space_constraint(v, pltpu.HBM) for v in (step_choices, pattern, density)))
 
 
 def solution(mesh):

time: 74 us -> 72.9 us (0.985)
  local copies, waits for them, and re-layouts: 2.08 us -> 1.17 us
    unnamed x4 -> x2, local copies, waits for them, and re-layouts: 2.08 us -> 1.17 us
where the time goes in v5:
time: 72.9 us; the launch traced here: 72.8 us
  Pallas kernels  71 us (97%)
  local copies, waits for them, and re-layouts  1.17 us (2%)
    pallas_call x1, Pallas kernels, shards(): pl.pallas_call(kernel, out_shape=(jax.ShapeDtypeStruct(density.shape, F32...  71 us

profile of v5, /device:TPU:1, one launch (start us, length us, event | category | flops | bytes accessed | tf_op | source)
XLA Modules:
  0.0 72.8 jit_solution(3363628559040195118)
XLA Ops:
  0.6 71.0 %shard_map.50 = (f32[128,256]{1,0:T(8,128)S(1)}, f32[2]{0:T(128)S(1)}) custom-call(s32[2]{0:T(128)} %choice_hbm.1, s32[1,2]{1,0:T(1,128)} %pat_hbm.1, f32[128,256]{1,0:T(8,128)} %x_ref.1), custom_call_target="tpu_custom_call" | custom-call | tf_op jit(solution)/shard_map/pallas_call | solution.py:310
  71.6 0.7 copy.7
  72.3 0.5 copy.8

commit v6 on v5

--- a/solution.py
+++ b/solution.py
@@ -292,8 +292,7 @@
         return 0
 
     lax.fori_loop(0, STEPS, advance, 0)
-    store = pltpu.make_async_copy(bbuf.at[STEPS, bkey(0, 0)], out_ref, fetch_sem.at[0])
-    store.start()
+    out_ref[...] = bbuf[STEPS, bkey(0, 0)]
     for stage in range(len(groups)):
         for copy in tr_copies(stage):
             copy.wait_send()
@@ -301,7 +300,6 @@
         w = choice_ref[step].astype(F32)
         square, plain = jnp.sum(sums[4, 2 * step: 2 * step + 1]), jnp.sum(sums[4, 2 * step + 1: 2 * step + 2])
         tr_ref[step] = (1.0 - 2.0 * w) * square + 2.0 * w * plain
-    store.wait()
 
 
 def shards(density, pattern, step_choices):
@@ -311,7 +309,7 @@
         kernel,
         out_shape=(jax.ShapeDtypeStruct(density.shape, F32), jax.ShapeDtypeStruct((STEPS,), F32)),
         in_specs=[pl.BlockSpec(memory_space=pltpu.HBM)] * 3,
-        out_specs=(pl.BlockSpec(memory_space=pl.ANY), smem),
+        out_specs=(pl.BlockSpec(memory_space=pltpu.VMEM), smem),
         scratch_shapes=[
             pltpu.VMEM((STEPS, NK, 2 * B, B), F32),
             pltpu.VMEM((STEPS + 1, NK, B, 2 * B), F32),

time: 72.9 us -> 72.7 us (level)
  no operation moved by 1% of the time
where the time goes in v6:
time: 72.7 us; the launch traced here: 72.6 us
  Pallas kernels  70.8 us (97%)
  local copies, waits for them, and re-layouts  1.17 us (2%)
    pallas_call x1, Pallas kernels, shards(): pl.pallas_call(kernel, out_shape=(jax.ShapeDtypeStruct(density.shape, F32...  70.8 us

profile of v6, /device:TPU:1, one launch (start us, length us, event | category | flops | bytes accessed | tf_op | source)
XLA Modules:
  0.0 72.6 jit_solution(18087881562464400423)
XLA Ops:
  0.6 70.8 %shard_map.50 = (f32[128,256]{1,0:T(8,128)S(1)}, f32[2]{0:T(128)S(1)}) custom-call(s32[2]{0:T(128)} %choice_hbm.1, s32[1,2]{1,0:T(1,128)} %pat_hbm.1, f32[128,256]{1,0:T(8,128)} %x_ref.1), custom_call_target="tpu_custom_call" | custom-call | tf_op jit(solution)/shard_map/pallas_call | solution.py:308
  71.4 0.7 copy.7
  72.1 0.5 copy.8
